TPU v7x, 32 devices: a whole 2x2x4 slice. The times are simulated.
32 devices in a mesh: groups: 2 (over y), tap: 4 (over z), tm: 2 (over x), lag: 2 (over core).
Axes of the slice: x: 2, y: 2, z: 4, core: 2. Of those that a mesh axis runs over, the one named last changes fastest.
Arguments:
- raw_strain: bfloat16 [2048, 1024], P(('groups', 'tap'), 'tm'), parts along dimension 0, may hold values from -4000 to 4000
- spatial_filter: float32 [33], replicated, may hold values from -0.35 to 0.35
- temporal_filter: float32 [255], replicated, may hold values from -0.125 to 0.125
- dest_blocks: int32 [16, 2], P('groups'), parts along dimension 0, may hold values from 0 to 7, as said below
- partner_codes: int32 [16, 128, 64], P(('groups', 'tap', 'lag'), 'tm'), parts along dimension 0, may hold values from 0 to 255, as said below
Outputs:
- coherence: bfloat16 [16, 128, 64, 512], P(('groups', 'tap', 'lag'), 'tm'), parts along dimension 0
There are 2 independent parts, one for each index of `groups`. A program takes and returns all parts, laid end to end along the dimension named above; an argument that names none is the same for every part. Nothing has to cross between parts.
Inputs may be any that keep to these rules, and one draw needn't show every extreme that they name: With n the number of devices along lag, the values dest_blocks[s, j] // n of one row s are distinct and all differ from s // n. `partner_codes`: the 64 codes of one source tap are distinct. Within every source block, each destination slot 0 .. 1 is named by the codes of some tap of that block.
All inputs are finite; a program needn't handle non-finite values.
Results may differ from a plain program's by a relative error of at most 0.022.
Values may be sent and summed in bfloat16 or wider, within the bound.
No kernel may reach another device: no remote copies, remote signals or barrier semaphores. Data moves between devices by JAX's collectives and lax.ppermute only.
A program may use at most 128 MiB of HBM per device.

v0:
```python
import math
import jax
import jax.numpy as jnp
from jax import lax
from jax.sharding import PartitionSpec as P

LAG_COUNT = 512
EPSILON = 1e-06


def extended(cells, sides, width):
    for axis, dim in sides:
        count = lax.axis_size(axis)
        ends = count - 1
        head = lax.slice_in_dim(cells, 0, width, axis=dim)
        tail = lax.slice_in_dim(cells, cells.shape[dim] - width, cells.shape[dim], axis=dim)
        cells = jnp.concatenate(
            [
                lax.ppermute(tail, axis, [(i, (i + 1) % count) for i in range(ends)]),
                cells,
                lax.ppermute(head, axis, [((i + 1) % count, i) for i in range(ends)]),
            ],
            axis=dim,
        )
    return cells


def band_matrix(vector, row_count, col_count):
    length = vector.shape[0]
    padded = jnp.concatenate([vector, jnp.zeros((col_count + 1 - length,), vector.dtype)])
    repeated = jnp.tile(padded, row_count)[: row_count * col_count]
    return repeated.reshape(row_count, col_count)


def split_parts(matrix):
    high_part = matrix.astype(jnp.bfloat16)
    low_part = (matrix - high_part.astype(jnp.float32)).astype(jnp.bfloat16)
    return (high_part, low_part)


def whiten(strain_ext, row_count, spatial_filter, temporal_filter):
    spatial = band_matrix(spatial_filter, row_count, strain_ext.shape[0])
    spatial_high, spatial_low = split_parts(spatial)
    smooth = jnp.einsum("cr,rt->ct", spatial_high, strain_ext, preferred_element_type=jnp.float32)
    smooth = smooth + jnp.einsum(
        "cr,rt->ct", spatial_low, strain_ext, preferred_element_type=jnp.float32
    )
    smooth = smooth.astype(jnp.bfloat16)
    time_half = temporal_filter.shape[0] // 2
    smooth_ext = extended(smooth, (("tm", 1),), time_half)
    temporal = band_matrix(temporal_filter, smooth.shape[1], smooth_ext.shape[1])
    temporal_high, temporal_low = split_parts(temporal)
    whitened = jnp.einsum(
        "cs,ts->ct", smooth_ext, temporal_high, preferred_element_type=jnp.float32
    )
    whitened = whitened + jnp.einsum(
        "cs,ts->ct", smooth_ext, temporal_low, preferred_element_type=jnp.float32
    )
    return whitened.astype(jnp.bfloat16)


def lag_products(buffer, own_row, row_index, lag_count):
    time_total = own_row.shape[0]
    lag_tile = lag_count // 4
    lag_half = lag_count // 2
    picked = jnp.take(buffer, row_index, axis=0)
    padded = jnp.pad(picked, ((0, 0), (lag_half, lag_half)))
    shifted = jnp.concatenate(
        [
            padded[:, shift_step * lag_tile : shift_step * lag_tile + time_total + lag_tile]
            for shift_step in range(4)
        ],
        axis=0,
    )
    toeplitz = band_matrix(own_row, lag_tile, time_total + lag_tile)
    products = lax.dot_general(
        shifted, toeplitz, (((1,), (1,)), ((), ())), preferred_element_type=jnp.float32
    )
    return products.reshape(4, -1, lag_tile).transpose(1, 0, 2).reshape(-1, lag_count)


def per_device(raw_strain, spatial_filter, temporal_filter, dest_blocks, partner_codes):
    taps_here, steps_time = raw_strain.shape
    lag_devices = lax.axis_size("lag")
    tap_devices = lax.axis_size("tap")
    time_devices = lax.axis_size("tm")
    block_taps = taps_here // lag_devices
    lag_index = lax.axis_index("lag")
    tap_index = lax.axis_index("tap")
    spatial_halfwidth = spatial_filter.shape[0] // 2
    strain_ext = extended(raw_strain, (("tap", 0),), spatial_halfwidth)
    whitened = whiten(strain_ext, taps_here, spatial_filter, temporal_filter)
    dest_count = dest_blocks.shape[1]
    by_owner = dest_blocks.reshape(tap_devices, lag_devices, dest_count)
    requests = lax.dynamic_index_in_dim(by_owner, lag_index, 1, keepdims=False)
    req_owner = requests // lag_devices
    req_local = requests % lag_devices
    owner_match = req_owner == tap_index
    local_match = req_local[:, :, None] == jnp.arange(lag_devices, dtype=jnp.int32)[None, None, :]
    selector = jnp.sum(
        jnp.logical_and(owner_match[:, :, None], local_match).astype(jnp.float32), axis=1
    )
    blocks_here = whitened.reshape(lag_devices, block_taps, steps_time)
    outgoing = jnp.einsum(
        "il,lbt->ibt",
        selector.astype(jnp.bfloat16),
        blocks_here,
        preferred_element_type=jnp.float32,
    ).astype(jnp.bfloat16)
    my_blocks = lax.dynamic_index_in_dim(requests, tap_index, 0, keepdims=False)
    my_owners = my_blocks // lag_devices
    code_table = partner_codes[0]
    spread_out = jnp.broadcast_to(
        outgoing[:, None], (tap_devices, time_devices, block_taps, steps_time)
    )
    spread_out = spread_out.reshape(tap_devices * time_devices, block_taps, steps_time)
    arrived = lax.all_to_all(spread_out, ("tap", "tm"), split_axis=0, concat_axis=2, tiled=True)
    arrived = arrived.reshape(block_taps, tap_devices, time_devices * steps_time)
    picked = jnp.take(arrived, my_owners, axis=1)
    buffer = picked.reshape(block_taps * dest_count, -1)
    row_index = code_table % block_taps * dest_count + code_table // block_taps
    own_block = lax.dynamic_slice_in_dim(whitened, lag_index * block_taps, block_taps, 0)
    own_rows = lax.all_to_all(own_block, "tm", split_axis=0, concat_axis=1, tiled=True)
    time_total = own_rows.shape[1]
    energy_own = jnp.sum(jnp.square(own_rows.astype(jnp.float32)), axis=1) / time_total + EPSILON
    energy_buffer = jnp.sum(jnp.square(buffer.astype(jnp.float32)), axis=1) / time_total + EPSILON
    energy_partner = jnp.take(energy_buffer, row_index)
    source_count = own_rows.shape[0]
    partner_count = row_index.shape[1]
    group_size = math.gcd(source_count, 8)
    rows_grouped = own_rows.reshape(source_count // group_size, group_size, time_total)
    index_grouped = row_index.reshape(source_count // group_size, group_size, partner_count)

    def tap_lag_offsets(own_row, indices):
        return lag_products(buffer, own_row, indices, LAG_COUNT)

    def group_products(pieces):
        return jax.vmap(tap_lag_offsets)(pieces[0], pieces[1])

    products = lax.map(group_products, (rows_grouped, index_grouped))
    products = products.reshape(source_count, partner_count, LAG_COUNT)
    norm_scale = jnp.sqrt(energy_own[:, None] * energy_partner) * jnp.sqrt(jnp.float32(time_total))
    coherence = (products / norm_scale[:, :, None]).astype(jnp.bfloat16)
    return coherence[None]


def solution(mesh):
    placed = (
        P(("groups", "tap"), "tm"),
        P(),
        P(),
        P("groups", None),
        P(("groups", "tap", "lag"), "tm", None),
    )
    return jax.shard_map(
        per_device,
        mesh=mesh,
        in_specs=placed,
        out_specs=P(("groups", "tap", "lag"), "tm", None, None),
        check_vma=False,
    )
```

profile of v0, /device:TPU:0, one launch (start us, length us, event | category | flops | bytes accessed | tf_op | source)
XLA Modules:
  0.0 268.1 jit_solution(12425569988358387064)
XLA Ops:
  2.6 6.2 %collective-permute-start = (bf16[16,512]{1,0:T(8,128)(2,1)}, bf16[16,512]{1,0:T(8,128)(2,1)}, u32[]{:S(2)}, u32[]{:S(2)}) collective-permute-start(bf16[16,512]{1,0:T(8,128)(2,1)} %get-tuple-element.88), channel_id=1, source_target_pairs={{0,4},{4,8},{8,12},{1,5},{5,9},{9,13},{2,6},{6,10},{10,14},{3,7},{... | collective-permute-start | bytes 49160 | tf_op jit(solution)/shard_map/ppermute | solution.py:19
  19.7 3.9 %collective-permute-start.2 = (bf16[256,127]{1,0:T(8,128)(2,1)S(1)}, bf16[256,127]{1,0:T(8,128)(2,1)S(1)}, u32[]{:S(2)}, u32[]{:S(2)}) collective-permute-start(bf16[256,127]{1,0:T(8,128)(2,1)S(1)} %get-tuple-element.85), channel_id=1, source_target_pairs={{0,2},{1,3},{4,6},{5,7},{8,10},{9,11},{12,14},{13,15},{16,18},{17,... | collective-permute-start | bytes 195080 | tf_op jit(solution)/shard_map/ppermute | solution.py:19
  25.4 4.3 %collective-permute-done.3 = bf16[256,127]{1,0:T(8,128)(2,1)S(1)} collective-permute-done((bf16[256,127]{1,0:T(8,128)(2,1)S(1)}, bf16[256,127]{1,0:T(8,128)(2,1)S(1)}, u32[]{:S(2)}, u32[]{:S(2)}) %collective-permute-start.3) | collective-permute-done | bytes 65056 | tf_op jit(solution)/shard_map/ppermute | solution.py:21
  40.2 3.8 %all-to-all-start = ((bf16[8,128,512]{1,2,0:T(8,128)(2,1)}), bf16[8,128,512]{1,2,0:T(8,128)(2,1)S(1)}, u32[]{:S(2)}, u32[]{:S(2)}) async-start(bf16[8,128,512]{1,2,0:T(8,128)(2,1)} %bitcast.9), calls=%async_computation | async-start | bytes 2097152 | tf_op jit(solution)/shard_map/all_to_all | solution.py:117
  45.0 21.9 %all-to-all-done = bf16[8,128,512]{1,2,0:T(8,128)(2,1)S(1)} async-done(((bf16[8,128,512]{1,2,0:T(8,128)(2,1)}), bf16[8,128,512]{1,2,0:T(8,128)(2,1)S(1)}, u32[]{:S(2)}, u32[]{:S(2)}) %all-to-all-start) | async-done | bytes 1048608 | tf_op jit(solution)/shard_map/all_to_all | solution.py:117
  68.6 25.7 %gather_fusion.2 = f32[4096]{0:T(1024)S(1)} fusion(f32[256]{0:T(256)S(1)} %add.219, s32[4096]{0:T(1024)S(1)} %broadcast_clamp_fusion), kind=kCustom, calls=%fused_computation.2 | custom fusion | bytes 49152 | tf_op jit(solution)/shard_map/jit(_take)/gather | solution.py:127
  95.3 167.5 %while.12 = (s32[]{:T(128)}, f32[8,8,64,512]{3,2,1,0:T(8,128)}, s32[8,8,64]{2,1,0:T(8,128)S(1)}, bf16[256,1024]{1,0:T(8,128)(2,1)S(1)}, bf16[8,8,1024]{2,1,0:T(8,128)(2,1)S(1)}, /*index=5*/s32[]{:T(128)}, bf16[]{:T(256)}) while((s32[]{:T(128)}, f32[8,8,64,512]{3,2,1,0:T(8,128)}, s32[8,8,64]{2,1,0:T(8,128)S(1)}, ...), condition=%wide.region_2.3_spmd, body=%wide.region_1.2_spmd.sunk | while | flops 623384064 | bytes 57009364 | solution.py:140
  99.1 5.2 %reshape.464 = bf16[1180672]{0:T(1024)(128)(2,1)} reshape(bf16[8,128,1153]{2,1,0:T(8,128)(2,1)S(1)} %tile.36) | data formatting | bytes 4722688 | tf_op jit(solution)/shard_map/while
  104.3 4.2 %tile.37 = bf16[8,147584]{1,0:T(8,128)(2,1)S(1)} reshape(bf16[1180672]{0:T(1024)(128)(2,1)} %reshape.464) | data formatting | bytes 4722688 | tf_op jit(solution)/shard_map/while/body/eval_jaxpr/vmap()/tile | solution.py:31
  119.9 5.2 %reshape.464 = bf16[1180672]{0:T(1024)(128)(2,1)} reshape(bf16[8,128,1153]{2,1,0:T(8,128)(2,1)S(1)} %tile.36) | data formatting | bytes 4722688 | tf_op jit(solution)/shard_map/while
  125.2 4.2 %tile.37 = bf16[8,147584]{1,0:T(8,128)(2,1)S(1)} reshape(bf16[1180672]{0:T(1024)(128)(2,1)} %reshape.464) | data formatting | bytes 4722688 | tf_op jit(solution)/shard_map/while/body/eval_jaxpr/vmap()/tile | solution.py:31
  140.9 5.2 %reshape.464 = bf16[1180672]{0:T(1024)(128)(2,1)} reshape(bf16[8,128,1153]{2,1,0:T(8,128)(2,1)S(1)} %tile.36) | data formatting | bytes 4722688 | tf_op jit(solution)/shard_map/while
  146.1 4.2 %tile.37 = bf16[8,147584]{1,0:T(8,128)(2,1)S(1)} reshape(bf16[1180672]{0:T(1024)(128)(2,1)} %reshape.464) | data formatting | bytes 4722688 | tf_op jit(solution)/shard_map/while/body/eval_jaxpr/vmap()/tile | solution.py:31
  161.8 5.2 %reshape.464 = bf16[1180672]{0:T(1024)(128)(2,1)} reshape(bf16[8,128,1153]{2,1,0:T(8,128)(2,1)S(1)} %tile.36) | data formatting | bytes 4722688 | tf_op jit(solution)/shard_map/while
  167.0 4.2 %tile.37 = bf16[8,147584]{1,0:T(8,128)(2,1)S(1)} reshape(bf16[1180672]{0:T(1024)(128)(2,1)} %reshape.464) | data formatting | bytes 4722688 | tf_op jit(solution)/shard_map/while/body/eval_jaxpr/vmap()/tile | solution.py:31
  182.7 5.2 %reshape.464 = bf16[1180672]{0:T(1024)(128)(2,1)} reshape(bf16[8,128,1153]{2,1,0:T(8,128)(2,1)S(1)} %tile.36) | data formatting | bytes 4722688 | tf_op jit(solution)/shard_map/while
  187.9 4.2 %tile.37 = bf16[8,147584]{1,0:T(8,128)(2,1)S(1)} reshape(bf16[1180672]{0:T(1024)(128)(2,1)} %reshape.464) | data formatting | bytes 4722688 | tf_op jit(solution)/shard_map/while/body/eval_jaxpr/vmap()/tile | solution.py:31
  203.6 5.2 %reshape.464 = bf16[1180672]{0:T(1024)(128)(2,1)} reshape(bf16[8,128,1153]{2,1,0:T(8,128)(2,1)S(1)} %tile.36) | data formatting | bytes 4722688 | tf_op jit(solution)/shard_map/while
  208.8 4.2 %tile.37 = bf16[8,147584]{1,0:T(8,128)(2,1)S(1)} reshape(bf16[1180672]{0:T(1024)(128)(2,1)} %reshape.464) | data formatting | bytes 4722688 | tf_op jit(solution)/shard_map/while/body/eval_jaxpr/vmap()/tile | solution.py:31
  224.5 5.2 %reshape.464 = bf16[1180672]{0:T(1024)(128)(2,1)} reshape(bf16[8,128,1153]{2,1,0:T(8,128)(2,1)S(1)} %tile.36) | data formatting | bytes 4722688 | tf_op jit(solution)/shard_map/while
  229.7 4.2 %tile.37 = bf16[8,147584]{1,0:T(8,128)(2,1)S(1)} reshape(bf16[1180672]{0:T(1024)(128)(2,1)} %reshape.464) | data formatting | bytes 4722688 | tf_op jit(solution)/shard_map/while/body/eval_jaxpr/vmap()/tile | solution.py:31
  245.4 5.2 %reshape.464 = bf16[1180672]{0:T(1024)(128)(2,1)} reshape(bf16[8,128,1153]{2,1,0:T(8,128)(2,1)S(1)} %tile.36) | data formatting | bytes 4722688 | tf_op jit(solution)/shard_map/while
  250.7 4.2 %tile.37 = bf16[8,147584]{1,0:T(8,128)(2,1)S(1)} reshape(bf16[1180672]{0:T(1024)(128)(2,1)} %reshape.464) | data formatting | bytes 4722688 | tf_op jit(solution)/shard_map/while/body/eval_jaxpr/vmap()/tile | solution.py:31
  262.9 5.2 %fusion.11 = bf16[1,64,64,512]{3,2,1,0:T(8,128)(2,1)} fusion(f32[64,64]{1,0:T(8,128)S(1)} %sqrt_multiply_fusion, f32[1,64,64,512]{3,2,1,0:T(8,128)} %bitcast.135), kind=kLoop, calls=%fused_computation.26 | loop fusion | flops 4194304 | bytes 12599296 | tf_op jit(solution)/shard_map/convert_element_type | solution.py:143
  (225 shorter events, 120.5 us)
Async XLA Ops:
  1.3 16.9 %collective-permute-start.1 = (bf16[16,512]{1,0:T(8,128)(2,1)}, bf16[16,512]{1,0:T(8,128)(2,1)}, u32[]{:S(2)}, u32[]{:S(2)}) collective-permute-start(bf16[16,512]{1,0:T(8,128)(2,1)} %get-tuple-element.87), channel_id=1, source_target_pairs={{4,0},{8,4},{12,8},{5,1},{9,5},{13,9},{6,2},{10,6},{14,10},{7,3},{... | collective-permute-start | bytes 49160 | tf_op jit(solution)/shard_map/ppermute | solution.py:21
  2.6 14.9 %collective-permute-start = (bf16[16,512]{1,0:T(8,128)(2,1)}, bf16[16,512]{1,0:T(8,128)(2,1)}, u32[]{:S(2)}, u32[]{:S(2)}) collective-permute-start(bf16[16,512]{1,0:T(8,128)(2,1)} %get-tuple-element.88), channel_id=1, source_target_pairs={{0,4},{4,8},{8,12},{1,5},{5,9},{9,13},{2,6},{6,10},{10,14},{3,7},{... | collective-permute-start | bytes 49160 | tf_op jit(solution)/shard_map/ppermute | solution.py:19
  14.4 3.9 %copy-start.2 = (bf16[256,512]{1,0:T(8,128)(2,1)S(1)}, bf16[256,512]{1,0:T(8,128)(2,1)}, u32[]{:S(2)}) copy-start(bf16[256,512]{1,0:T(8,128)(2,1)} %param.7) | copy-start | bytes 786436
  19.7 5.7 %collective-permute-start.2 = (bf16[256,127]{1,0:T(8,128)(2,1)S(1)}, bf16[256,127]{1,0:T(8,128)(2,1)S(1)}, u32[]{:S(2)}, u32[]{:S(2)}) collective-permute-start(bf16[256,127]{1,0:T(8,128)(2,1)S(1)} %get-tuple-element.85), channel_id=1, source_target_pairs={{0,2},{1,3},{4,6},{5,7},{8,10},{9,11},{12,14},{13,15},{16,18},{17,... | collective-permute-start | bytes 195080 | tf_op jit(solution)/shard_map/ppermute | solution.py:19
  23.6 6.2 %collective-permute-start.3 = (bf16[256,127]{1,0:T(8,128)(2,1)S(1)}, bf16[256,127]{1,0:T(8,128)(2,1)S(1)}, u32[]{:S(2)}, u32[]{:S(2)}) collective-permute-start(bf16[256,127]{1,0:T(8,128)(2,1)S(1)} %get-tuple-element.86), channel_id=1, source_target_pairs={{2,0},{3,1},{6,4},{7,5},{10,8},{11,9},{14,12},{15,13},{18,16},{19,... | collective-permute-start | bytes 195080 | tf_op jit(solution)/shard_map/ppermute | solution.py:21
  31.2 7.8 %all-to-all-start.1 = ((bf16[2,64,512]{2,1,0:T(8,128)(2,1)}), bf16[2,64,512]{2,1,0:T(8,128)(2,1)S(1)}, u32[]{:S(2)}, u32[]{:S(2)}) async-start(bf16[2,64,512]{2,1,0:T(8,128)(2,1)} %bitcast.15), calls=%async_computation.1 | async-start | bytes 262144 | tf_op jit(solution)/shard_map/all_to_all | solution.py:123
  35.1 9.3 %copy-start.3 = (s32[1,64,64]{2,1,0:T(8,128)S(1)}, s32[1,64,64]{2,1,0:T(8,128)}, u32[]{:S(2)}) copy-start(s32[1,64,64]{2,1,0:T(8,128)} %param.11) | copy-start | bytes 49156
  40.2 26.7 %all-to-all-start = ((bf16[8,128,512]{1,2,0:T(8,128)(2,1)}), bf16[8,128,512]{1,2,0:T(8,128)(2,1)S(1)}, u32[]{:S(2)}, u32[]{:S(2)}) async-start(bf16[8,128,512]{1,2,0:T(8,128)(2,1)} %bitcast.9), calls=%async_computation | async-start | bytes 2097152 | tf_op jit(solution)/shard_map/all_to_all | solution.py:117
  108.5 2.0 copy-start.1
  110.5 1.7 slice-start
  129.4 2.0 copy-start.1
  131.4 1.7 slice-start
  150.3 2.0 copy-start.1
  152.4 1.7 slice-start
  171.3 2.0 copy-start.1
  173.3 1.7 slice-start
  192.2 2.0 copy-start.1
  194.2 1.7 slice-start
  213.1 2.0 copy-start.1
  215.1 1.7 slice-start
  234.0 2.0 copy-start.1
  236.0 1.7 slice-start
  254.9 2.0 copy-start.1
  256.9 1.7 slice-start
  (8 other events, 11.3 us)
where the time goes:
time: 270 us; the launch traced here: 268 us
  local copies, waits for them, and re-layouts  183 us (68%)
  waiting for transfers between devices  30.3 us (11%)
  starting transfers between devices  19.8 us (7%)
  matrix products  17.7 us (7%)
  other arithmetic  15.9 us (6%)
    while x40, local copies, waits for them, and re-layouts  57.8 us
    another operation x20, local copies, waits for them, and re-layouts, band_matrix(): repeated = jnp.tile(padded, row_count)[:row_count * col_count]  36.9 us
    gather x2, local copies, waits for them, and re-layouts, per_device(): energy_partner = jnp.take(energy_buffer, row_index)  25.8 us
    all_to_all x1, waiting for transfers between devices, per_device(): lax.all_to_all(spread_out, ('tap', 'tm'), split_axis=0, concat_axis=2, ti...  21.9 us
    gather x8, local copies, waits for them, and re-layouts, lag_products(): picked = jnp.take(buffer, row_index, axis=0)  16.5 us
    dot_general x8, matrix products, lag_products(): lax.dot_general(shifted, toeplitz, (((1,), (1,)), ((), ())), preferred_el...  15.8 us
    ppermute x2, starting transfers between devices, extended(): lax.ppermute(tail, axis, [(i, (i + 1) % count) for i in range(ends)])  10 us
    select_n x16, other arithmetic, lag_products(): picked = jnp.take(buffer, row_index, axis=0)  9.78 us
  transfers between devices with their start and end apart: 6, of which 4 were waited for; matrix products, arithmetic and copies ran while one was open for 4% of the time, Pallas kernels for 0%

commit v1 on v0

--- a/solution.py
+++ b/solution.py
@@ -120,7 +120,10 @@
     buffer = picked.reshape(block_taps * dest_count, -1)
     row_index = code_table % block_taps * dest_count + code_table // block_taps
     own_block = lax.dynamic_slice_in_dim(whitened, lag_index * block_taps, block_taps, 0)
-    own_rows = lax.all_to_all(own_block, "tm", split_axis=0, concat_axis=1, tiled=True)
+    own_rows = jnp.concatenate(
+        lax.all_to_all(jnp.stack(jnp.split(own_block, lax.axis_size("tm"), axis=0)), "tm", 0, 0),
+        axis=1,
+    )
     time_total = own_rows.shape[1]
     energy_own = jnp.sum(jnp.square(own_rows.astype(jnp.float32)), axis=1) / time_total + EPSILON
     energy_buffer = jnp.sum(jnp.square(buffer.astype(jnp.float32)), axis=1) / time_total + EPSILON

time: 270 us -> 269 us (level)
  no operation moved by 1% of the time
where the time goes in v1:
time: 269 us; the launch traced here: 268 us
  local copies, waits for them, and re-layouts  183 us (68%)
  waiting for transfers between devices  30.3 us (11%)
  starting transfers between devices  19.8 us (7%)
  matrix products  17.7 us (7%)
  other arithmetic  16.5 us (6%)
    while x40, local copies, waits for them, and re-layouts  57.8 us
    another operation x20, local copies, waits for them, and re-layouts, band_matrix(): repeated = jnp.tile(padded, row_count)[:row_count * col_count]  36.9 us
    gather x2, local copies, waits for them, and re-layouts, per_device(): energy_partner = jnp.take(energy_buffer, row_index)  25.8 us
    all_to_all x1, waiting for transfers between devices, per_device(): lax.all_to_all(spread_out, ('tap', 'tm'), split_axis=0, concat_axis=2, ti...  21.9 us
    gather x8, local copies, waits for them, and re-layouts, lag_products(): picked = jnp.take(buffer, row_index, axis=0)  16.5 us
    dot_general x8, matrix products, lag_products(): lax.dot_general(shifted, toeplitz, (((1,), (1,)), ((), ())), preferred_el...  15.8 us
    ppermute x2, starting transfers between devices, extended(): lax.ppermute(tail, axis, [(i, (i + 1) % count) for i in range(ends)])  9.98 us
    select_n x16, other arithmetic, lag_products(): picked = jnp.take(buffer, row_index, axis=0)  9.71 us
  transfers between devices with their start and end apart: 6, of which 4 were waited for; matrix products, arithmetic and copies ran while one was open for 4% of the time, Pallas kernels for 0%

profile of v1, /device:TPU:0, one launch (start us, length us, event | category | flops | bytes accessed | tf_op | source)
XLA Modules:
  0.0 268.0 jit_solution(11840539511501396997)
XLA Ops:
  2.6 6.2 %collective-permute-start = (bf16[16,512]{1,0:T(8,128)(2,1)}, bf16[16,512]{1,0:T(8,128)(2,1)}, u32[]{:S(2)}, u32[]{:S(2)}) collective-permute-start(bf16[16,512]{1,0:T(8,128)(2,1)} %get-tuple-element.90), channel_id=1, source_target_pairs={{0,4},{4,8},{8,12},{1,5},{5,9},{9,13},{2,6},{6,10},{10,14},{3,7},{... | collective-permute-start | bytes 49160 | tf_op jit(solution)/shard_map/ppermute | solution.py:19
  19.7 3.8 %collective-permute-start.2 = (bf16[256,127]{1,0:T(8,128)(2,1)S(1)}, bf16[256,127]{1,0:T(8,128)(2,1)S(1)}, u32[]{:S(2)}, u32[]{:S(2)}) collective-permute-start(bf16[256,127]{1,0:T(8,128)(2,1)S(1)} %get-tuple-element.87), channel_id=1, source_target_pairs={{0,2},{1,3},{4,6},{5,7},{8,10},{9,11},{12,14},{13,15},{16,18},{17,... | collective-permute-start | bytes 195080 | tf_op jit(solution)/shard_map/ppermute | solution.py:19
  25.4 4.3 %collective-permute-done.3 = bf16[256,127]{1,0:T(8,128)(2,1)S(1)} collective-permute-done((bf16[256,127]{1,0:T(8,128)(2,1)S(1)}, bf16[256,127]{1,0:T(8,128)(2,1)S(1)}, u32[]{:S(2)}, u32[]{:S(2)}) %collective-permute-start.3) | collective-permute-done | bytes 65056 | tf_op jit(solution)/shard_map/ppermute | solution.py:21
  40.2 3.9 %all-to-all-start = ((bf16[8,128,512]{1,2,0:T(8,128)(2,1)}), bf16[8,128,512]{1,2,0:T(8,128)(2,1)S(1)}, u32[]{:S(2)}, u32[]{:S(2)}) async-start(bf16[8,128,512]{1,2,0:T(8,128)(2,1)} %bitcast.9), calls=%async_computation | async-start | bytes 2097152 | tf_op jit(solution)/shard_map/all_to_all | solution.py:117
  45.0 21.9 %all-to-all-done = bf16[8,128,512]{1,2,0:T(8,128)(2,1)S(1)} async-done(((bf16[8,128,512]{1,2,0:T(8,128)(2,1)}), bf16[8,128,512]{1,2,0:T(8,128)(2,1)S(1)}, u32[]{:S(2)}, u32[]{:S(2)}) %all-to-all-start) | async-done | bytes 1048608 | tf_op jit(solution)/shard_map/all_to_all | solution.py:117
  68.6 25.7 %gather_fusion.2 = f32[4096]{0:T(1024)S(1)} fusion(f32[256]{0:T(256)S(1)} %add.219, s32[4096]{0:T(1024)S(1)} %broadcast_clamp_fusion), kind=kCustom, calls=%fused_computation.2 | custom fusion | bytes 49152 | tf_op jit(solution)/shard_map/jit(_take)/gather | solution.py:130
  95.3 167.4 %while.12 = (s32[]{:T(128)}, f32[8,8,64,512]{3,2,1,0:T(8,128)}, s32[8,8,64]{2,1,0:T(8,128)S(1)}, bf16[256,1024]{1,0:T(8,128)(2,1)S(1)}, bf16[8,8,1024]{2,1,0:T(8,128)(2,1)S(1)}, /*index=5*/s32[]{:T(128)}, bf16[]{:T(256)}) while((s32[]{:T(128)}, f32[8,8,64,512]{3,2,1,0:T(8,128)}, s32[8,8,64]{2,1,0:T(8,128)S(1)}, ...), condition=%wide.region_2.3_spmd, body=%wide.region_1.2_spmd.sunk | while | flops 623384064 | bytes 57009364 | solution.py:143
  99.1 5.2 %reshape.461 = bf16[1180672]{0:T(1024)(128)(2,1)} reshape(bf16[8,128,1153]{2,1,0:T(8,128)(2,1)S(1)} %tile.36) | data formatting | bytes 4722688 | tf_op jit(solution)/shard_map/while
  104.3 4.2 %tile.37 = bf16[8,147584]{1,0:T(8,128)(2,1)S(1)} reshape(bf16[1180672]{0:T(1024)(128)(2,1)} %reshape.461) | data formatting | bytes 4722688 | tf_op jit(solution)/shard_map/while/body/eval_jaxpr/vmap()/tile | solution.py:31
  119.9 5.2 %reshape.461 = bf16[1180672]{0:T(1024)(128)(2,1)} reshape(bf16[8,128,1153]{2,1,0:T(8,128)(2,1)S(1)} %tile.36) | data formatting | bytes 4722688 | tf_op jit(solution)/shard_map/while
  125.2 4.2 %tile.37 = bf16[8,147584]{1,0:T(8,128)(2,1)S(1)} reshape(bf16[1180672]{0:T(1024)(128)(2,1)} %reshape.461) | data formatting | bytes 4722688 | tf_op jit(solution)/shard_map/while/body/eval_jaxpr/vmap()/tile | solution.py:31
  140.9 5.2 %reshape.461 = bf16[1180672]{0:T(1024)(128)(2,1)} reshape(bf16[8,128,1153]{2,1,0:T(8,128)(2,1)S(1)} %tile.36) | data formatting | bytes 4722688 | tf_op jit(solution)/shard_map/while
  146.1 4.2 %tile.37 = bf16[8,147584]{1,0:T(8,128)(2,1)S(1)} reshape(bf16[1180672]{0:T(1024)(128)(2,1)} %reshape.461) | data formatting | bytes 4722688 | tf_op jit(solution)/shard_map/while/body/eval_jaxpr/vmap()/tile | solution.py:31
  161.8 5.2 %reshape.461 = bf16[1180672]{0:T(1024)(128)(2,1)} reshape(bf16[8,128,1153]{2,1,0:T(8,128)(2,1)S(1)} %tile.36) | data formatting | bytes 4722688 | tf_op jit(solution)/shard_map/while
  167.0 4.2 %tile.37 = bf16[8,147584]{1,0:T(8,128)(2,1)S(1)} reshape(bf16[1180672]{0:T(1024)(128)(2,1)} %reshape.461) | data formatting | bytes 4722688 | tf_op jit(solution)/shard_map/while/body/eval_jaxpr/vmap()/tile | solution.py:31
  182.7 5.2 %reshape.461 = bf16[1180672]{0:T(1024)(128)(2,1)} reshape(bf16[8,128,1153]{2,1,0:T(8,128)(2,1)S(1)} %tile.36) | data formatting | bytes 4722688 | tf_op jit(solution)/shard_map/while
  187.9 4.2 %tile.37 = bf16[8,147584]{1,0:T(8,128)(2,1)S(1)} reshape(bf16[1180672]{0:T(1024)(128)(2,1)} %reshape.461) | data formatting | bytes 4722688 | tf_op jit(solution)/shard_map/while/body/eval_jaxpr/vmap()/tile | solution.py:31
  203.6 5.2 %reshape.461 = bf16[1180672]{0:T(1024)(128)(2,1)} reshape(bf16[8,128,1153]{2,1,0:T(8,128)(2,1)S(1)} %tile.36) | data formatting | bytes 4722688 | tf_op jit(solution)/shard_map/while
  208.8 4.2 %tile.37 = bf16[8,147584]{1,0:T(8,128)(2,1)S(1)} reshape(bf16[1180672]{0:T(1024)(128)(2,1)} %reshape.461) | data formatting | bytes 4722688 | tf_op jit(solution)/shard_map/while/body/eval_jaxpr/vmap()/tile | solution.py:31
  224.5 5.2 %reshape.461 = bf16[1180672]{0:T(1024)(128)(2,1)} reshape(bf16[8,128,1153]{2,1,0:T(8,128)(2,1)S(1)} %tile.36) | data formatting | bytes 4722688 | tf_op jit(solution)/shard_map/while
  229.7 4.2 %tile.37 = bf16[8,147584]{1,0:T(8,128)(2,1)S(1)} reshape(bf16[1180672]{0:T(1024)(128)(2,1)} %reshape.461) | data formatting | bytes 4722688 | tf_op jit(solution)/shard_map/while/body/eval_jaxpr/vmap()/tile | solution.py:31
  245.4 5.2 %reshape.461 = bf16[1180672]{0:T(1024)(128)(2,1)} reshape(bf16[8,128,1153]{2,1,0:T(8,128)(2,1)S(1)} %tile.36) | data formatting | bytes 4722688 | tf_op jit(solution)/shard_map/while
  250.6 4.2 %tile.37 = bf16[8,147584]{1,0:T(8,128)(2,1)S(1)} reshape(bf16[1180672]{0:T(1024)(128)(2,1)} %reshape.461) | data formatting | bytes 4722688 | tf_op jit(solution)/shard_map/while/body/eval_jaxpr/vmap()/tile | solution.py:31
  262.8 5.2 %fusion.11 = bf16[1,64,64,512]{3,2,1,0:T(8,128)(2,1)} fusion(f32[64,64]{1,0:T(8,128)S(1)} %sqrt_multiply_fusion, f32[1,64,64,512]{3,2,1,0:T(8,128)} %bitcast.138), kind=kLoop, calls=%fused_computation.26 | loop fusion | flops 4194304 | bytes 12599296 | tf_op jit(solution)/shard_map/convert_element_type | solution.py:146
  (226 shorter events, 120.4 us)
Async XLA Ops:
  1.3 16.9 %collective-permute-start.1 = (bf16[16,512]{1,0:T(8,128)(2,1)}, bf16[16,512]{1,0:T(8,128)(2,1)}, u32[]{:S(2)}, u32[]{:S(2)}) collective-permute-start(bf16[16,512]{1,0:T(8,128)(2,1)} %get-tuple-element.89), channel_id=1, source_target_pairs={{4,0},{8,4},{12,8},{5,1},{9,5},{13,9},{6,2},{10,6},{14,10},{7,3},{... | collective-permute-start | bytes 49160 | tf_op jit(solution)/shard_map/ppermute | solution.py:21
  2.6 14.9 %collective-permute-start = (bf16[16,512]{1,0:T(8,128)(2,1)}, bf16[16,512]{1,0:T(8,128)(2,1)}, u32[]{:S(2)}, u32[]{:S(2)}) collective-permute-start(bf16[16,512]{1,0:T(8,128)(2,1)} %get-tuple-element.90), channel_id=1, source_target_pairs={{0,4},{4,8},{8,12},{1,5},{5,9},{9,13},{2,6},{6,10},{10,14},{3,7},{... | collective-permute-start | bytes 49160 | tf_op jit(solution)/shard_map/ppermute | solution.py:19
  14.4 3.9 %copy-start.2 = (bf16[256,512]{1,0:T(8,128)(2,1)S(1)}, bf16[256,512]{1,0:T(8,128)(2,1)}, u32[]{:S(2)}) copy-start(bf16[256,512]{1,0:T(8,128)(2,1)} %param.7) | copy-start | bytes 786436
  19.7 5.7 %collective-permute-start.2 = (bf16[256,127]{1,0:T(8,128)(2,1)S(1)}, bf16[256,127]{1,0:T(8,128)(2,1)S(1)}, u32[]{:S(2)}, u32[]{:S(2)}) collective-permute-start(bf16[256,127]{1,0:T(8,128)(2,1)S(1)} %get-tuple-element.87), channel_id=1, source_target_pairs={{0,2},{1,3},{4,6},{5,7},{8,10},{9,11},{12,14},{13,15},{16,18},{17,... | collective-permute-start | bytes 195080 | tf_op jit(solution)/shard_map/ppermute | solution.py:19
  23.5 6.2 %collective-permute-start.3 = (bf16[256,127]{1,0:T(8,128)(2,1)S(1)}, bf16[256,127]{1,0:T(8,128)(2,1)S(1)}, u32[]{:S(2)}, u32[]{:S(2)}) collective-permute-start(bf16[256,127]{1,0:T(8,128)(2,1)S(1)} %get-tuple-element.88), channel_id=1, source_target_pairs={{2,0},{3,1},{6,4},{7,5},{10,8},{11,9},{14,12},{15,13},{18,16},{19,... | collective-permute-start | bytes 195080 | tf_op jit(solution)/shard_map/ppermute | solution.py:21
  31.2 7.8 %all-to-all-start.1 = ((bf16[2,64,512]{2,1,0:T(8,128)(2,1)}), bf16[2,64,512]{2,1,0:T(8,128)(2,1)S(1)}, u32[]{:S(2)}, u32[]{:S(2)}) async-start(bf16[2,64,512]{2,1,0:T(8,128)(2,1)} %pad_maximum_fusion.3), calls=%async_computation.1 | async-start | bytes 262144 | tf_op jit(solution)/shard_map/all_to_all | solution.py:124
  35.1 9.3 %copy-start.3 = (s32[1,64,64]{2,1,0:T(8,128)S(1)}, s32[1,64,64]{2,1,0:T(8,128)}, u32[]{:S(2)}) copy-start(s32[1,64,64]{2,1,0:T(8,128)} %param.11) | copy-start | bytes 49156
  40.2 26.7 %all-to-all-start = ((bf16[8,128,512]{1,2,0:T(8,128)(2,1)}), bf16[8,128,512]{1,2,0:T(8,128)(2,1)S(1)}, u32[]{:S(2)}, u32[]{:S(2)}) async-start(bf16[8,128,512]{1,2,0:T(8,128)(2,1)} %bitcast.9), calls=%async_computation | async-start | bytes 2097152 | tf_op jit(solution)/shard_map/all_to_all | solution.py:117
  108.5 2.0 copy-start.1
  110.5 1.7 slice-start
  129.4 2.0 copy-start.1
  131.4 1.7 slice-start
  150.3 2.0 copy-start.1
  152.3 1.7 slice-start
  171.2 2.0 copy-start.1
  173.2 1.7 slice-start
  192.1 2.0 copy-start.1
  194.1 1.7 slice-start
  213.0 2.0 copy-start.1
  215.0 1.7 slice-start
  233.9 2.0 copy-start.1
  235.9 1.7 slice-start
  254.8 2.0 copy-start.1
  256.9 1.7 slice-start
  (8 other events, 11.3 us)
